TPU v7x, 512 devices: a whole 4x8x8 slice. The times are simulated.
512 devices in a mesh: src: 16 (over y, core), tgt: 32 (over x, z).
Axes of the slice: x: 4, y: 8, z: 8, core: 2. Of those that a mesh axis runs over, the one named last changes fastest.
Arguments:
- noise: float32 [16384, 384], P(('src', 'tgt')), may hold values from -16 to 16
- data: float32 [32768, 384], P('tgt', 'src'), may hold values from -6 to 6
Outputs:
- velocity: float32 [16384, 384], P(('src', 'tgt'))
- target_potential: float32 [32768], P('tgt')
All inputs are finite; a program needn't handle non-finite values.
Results may differ from a plain program's by a relative error of at most 0.0003.
Values sent between devices are 32-bit elements; how exact they have to be, the bound alone decides.
No kernel may reach another device: no remote copies, remote signals or barrier semaphores. Data moves between devices by JAX's collectives and lax.ppermute only.
A program may use at most 64 MiB of HBM per device.

v0:
```python
import math
import jax
import jax.numpy as jnp
from jax import lax
from jax.sharding import PartitionSpec as P

ITERS = 3
EPS = 0.05


def row_merge(z_tile):
    local_top = jnp.max(z_tile, axis=1)
    top = lax.pmax(local_top, "tgt")
    total = lax.psum(jnp.sum(jnp.exp(z_tile - top[:, None]), axis=1), "tgt")
    return top + jnp.log(total)


def col_merge(z_tile):
    local_top = jnp.max(z_tile, axis=0)
    top = lax.pmax(local_top, "src")
    total = lax.psum(jnp.sum(jnp.exp(z_tile - top[None, :]), axis=0), "src")
    return top + jnp.log(total)


def per_device(noise, data):
    source_rows = lax.all_gather(noise, "tgt", axis=0, tiled=True)
    target_rows = lax.all_gather(data, "src", axis=1, tiled=True)
    feat_width = source_rows.shape[1]
    src_total = source_rows.shape[0] * lax.axis_size("src")
    tgt_total = target_rows.shape[0] * lax.axis_size("tgt")
    source_sq = jnp.sum(source_rows * source_rows, axis=1)
    target_sq = jnp.sum(target_rows * target_rows, axis=1)
    cross = jnp.dot(
        source_rows,
        target_rows.T,
        precision=lax.Precision.HIGHEST,
        preferred_element_type=jnp.float32,
    )
    cost_tile = (source_sq[:, None] + target_sq[None, :] - 2.0 * cross) / feat_width
    g_pot = jnp.zeros((target_rows.shape[0],), jnp.float32)
    for step_index in range(ITERS):
        f_pot = -EPS * (math.log(src_total) + row_merge((g_pot[None, :] - cost_tile) / EPS))
        g_pot = -EPS * (math.log(tgt_total) + col_merge((f_pot[:, None] - cost_tile) / EPS))
    z_final = (g_pot[None, :] - cost_tile) / EPS
    lrow = row_merge(z_final)
    weight = jnp.exp(z_final - lrow[:, None])
    own_rows = noise.shape[0]
    whole = lax.psum(
        jnp.dot(
            weight, target_rows, precision=lax.Precision.HIGHEST, preferred_element_type=jnp.float32
        ),
        "tgt",
    )
    bary = lax.dynamic_slice_in_dim(whole, lax.axis_index("tgt") * own_rows, own_rows, 0)
    return (bary - noise, g_pot)


def solution(mesh):
    placed = (P(("src", "tgt"), None), P("tgt", "src"))
    return jax.shard_map(
        per_device,
        mesh=mesh,
        in_specs=placed,
        out_specs=(P(("src", "tgt"), None), P("tgt")),
        check_vma=False,
    )
```

profile of v0, /device:TPU:8, one launch (start us, length us, event | category | flops | bytes accessed | tf_op | source)
XLA Modules:
  0.0 1082.2 jit_solution(13867403295693776282)
XLA Ops:
  7.2 0.0 all-gather.5.cloned.1.call-start
  7.2 0.7 all-gather.5.cloned.1.call-update
  7.9 0.0 all-gather.3.cloned.1.call-start
  7.9 0.7 all-gather.3.cloned.1.call-update
  8.6 0.0 all-reduce.2.cloned.1.call-start
  8.7 47.0 %all-gather.5.cloned.1.call-done = f32[1024,384]{0,1:T(8,128)} async-done(((f32[1024,24]{0,1:T(8,128)}), f32[1024,384]{0,1:T(8,128)}) %all-gather.5.cloned.1.call-update) | async-done | bytes 1572880 | tf_op jit(solution)/shard_map/all_gather | solution.py:27
  55.7 1.5 multiply_reduce_fusion
  57.3 84.2 %all-gather.3.cloned.1.call-done = f32[1024,384]{1,0:T(8,128)} async-done(((f32[32,384]{1,0:T(8,128)}), f32[1024,384]{1,0:T(8,128)}) %all-gather.3.cloned.1.call-update) | async-done | bytes 1572880 | tf_op jit(solution)/shard_map/all_gather | solution.py:26
  141.5 1.6 multiply_reduce_fusion.1
  143.1 10.5 fusion.3
  153.6 72.1 %pmax.49 = f32[1024]{0:T(1024)S(1)} all-reduce(f32[1024]{0:T(1024)S(1)} %get-tuple-element.2), channel_id=1, replica_groups=mesh['src'=16,'tgt'=32] {'tgt'}, use_global_device_ids=true, to_apply=%region_3.0 | all-reduce | flops 1024 | bytes 8192 | tf_op jit(solution)/shard_map/pmax | solution.py:13
  225.7 3.0 exponential_reduce_fusion.6
  228.7 69.6 %psum.56 = f32[1024]{0:T(1024)S(1)} all-reduce(f32[1024]{0:T(1024)S(1)} %exponential_reduce_fusion.6), channel_id=1, replica_groups=mesh['src'=16,'tgt'=32] {'tgt'}, use_global_device_ids=true, to_apply=%region_5.0 | all-reduce | flops 1024 | bytes 8192 | tf_op jit(solution)/shard_map/psum | solution.py:14
  298.4 2.7 fusion.4
  301.1 20.6 %pmax.50 = f32[1024]{0:T(1024)S(1)} all-reduce(f32[1024]{0:T(1024)S(1)} %fusion.4), channel_id=1, replica_groups=mesh['src'=16,'tgt'=32] {'src'}, use_global_device_ids=true, to_apply=%region_7.0 | all-reduce | flops 1024 | bytes 8192 | tf_op jit(solution)/shard_map/pmax | solution.py:20
  321.7 3.2 exponential_reduce_fusion.5
  324.8 23.6 %psum.57 = f32[1024]{0:T(1024)S(1)} all-reduce(f32[1024]{0:T(1024)S(1)} %exponential_reduce_fusion.5), channel_id=1, replica_groups=mesh['src'=16,'tgt'=32] {'src'}, use_global_device_ids=true, to_apply=%region_9.0 | all-reduce | flops 1024 | bytes 8192 | tf_op jit(solution)/shard_map/psum | solution.py:21
  348.4 2.7 fusion.5
  351.1 71.6 %pmax.51 = f32[1024]{0:T(1024)S(1)} all-reduce(f32[1024]{0:T(1024)S(1)} %fusion.5), channel_id=1, replica_groups=mesh['src'=16,'tgt'=32] {'tgt'}, use_global_device_ids=true, to_apply=%region_11.0 | all-reduce | flops 1024 | bytes 8192 | tf_op jit(solution)/shard_map/pmax | solution.py:13
  422.7 3.1 exponential_reduce_fusion.4
  425.8 69.6 %psum.58 = f32[1024]{0:T(1024)S(1)} all-reduce(f32[1024]{0:T(1024)S(1)} %exponential_reduce_fusion.4), channel_id=1, replica_groups=mesh['src'=16,'tgt'=32] {'tgt'}, use_global_device_ids=true, to_apply=%region_13.0 | all-reduce | flops 1024 | bytes 8192 | tf_op jit(solution)/shard_map/psum | solution.py:14
  495.5 2.7 fusion.6
  498.1 23.6 %pmax.52 = f32[1024]{0:T(1024)S(1)} all-reduce(f32[1024]{0:T(1024)S(1)} %fusion.6), channel_id=1, replica_groups=mesh['src'=16,'tgt'=32] {'src'}, use_global_device_ids=true, to_apply=%region_15.0 | all-reduce | flops 1024 | bytes 8192 | tf_op jit(solution)/shard_map/pmax | solution.py:20
  521.7 3.2 exponential_reduce_fusion.3
  524.9 23.6 %psum.59 = f32[1024]{0:T(1024)S(1)} all-reduce(f32[1024]{0:T(1024)S(1)} %exponential_reduce_fusion.3), channel_id=1, replica_groups=mesh['src'=16,'tgt'=32] {'src'}, use_global_device_ids=true, to_apply=%region_17.0 | all-reduce | flops 1024 | bytes 8192 | tf_op jit(solution)/shard_map/psum | solution.py:21
  548.4 2.7 fusion.7
  551.1 71.8 %pmax.53 = f32[1024]{0:T(1024)S(1)} all-reduce(f32[1024]{0:T(1024)S(1)} %fusion.7), channel_id=1, replica_groups=mesh['src'=16,'tgt'=32] {'tgt'}, use_global_device_ids=true, to_apply=%region_19.0 | all-reduce | flops 1024 | bytes 8192 | tf_op jit(solution)/shard_map/pmax | solution.py:13
  622.9 3.1 exponential_reduce_fusion.2
  626.0 69.7 %psum.60 = f32[1024]{0:T(1024)S(1)} all-reduce(f32[1024]{0:T(1024)S(1)} %exponential_reduce_fusion.2), channel_id=1, replica_groups=mesh['src'=16,'tgt'=32] {'tgt'}, use_global_device_ids=true, to_apply=%region_21.0 | all-reduce | flops 1024 | bytes 8192 | tf_op jit(solution)/shard_map/psum | solution.py:14
  695.7 2.7 fusion.8
  698.3 23.6 %pmax.54 = f32[1024]{0:T(1024)S(1)} all-reduce(f32[1024]{0:T(1024)S(1)} %fusion.8), channel_id=1, replica_groups=mesh['src'=16,'tgt'=32] {'src'}, use_global_device_ids=true, to_apply=%region_23.0 | all-reduce | flops 1024 | bytes 8192 | tf_op jit(solution)/shard_map/pmax | solution.py:20
  721.9 3.2 exponential_reduce_fusion.1
  725.1 23.6 %psum.61 = f32[1024]{0:T(1024)S(1)} all-reduce(f32[1024]{0:T(1024)S(1)} %exponential_reduce_fusion.1), channel_id=1, replica_groups=mesh['src'=16,'tgt'=32] {'src'}, use_global_device_ids=true, to_apply=%region_25.0 | all-reduce | flops 1024 | bytes 8192 | tf_op jit(solution)/shard_map/psum | solution.py:21
  748.6 0.0 copy-start.2
  748.6 0.0 copy-start
  748.6 2.8 fusion.9
  751.4 71.6 %pmax.55 = f32[1024]{0:T(1024)S(1)} all-reduce(f32[1024]{0:T(1024)S(1)} %fusion.9), channel_id=1, replica_groups=mesh['src'=16,'tgt'=32] {'tgt'}, use_global_device_ids=true, to_apply=%region_27.0 | all-reduce | flops 1024 | bytes 8192 | tf_op jit(solution)/shard_map/pmax | solution.py:13
  823.0 3.1 exponential_reduce_fusion
  826.1 69.7 %psum.62 = f32[1024]{0:T(1024)S(1)} all-reduce(f32[1024]{0:T(1024)S(1)} %exponential_reduce_fusion), channel_id=1, replica_groups=mesh['src'=16,'tgt'=32] {'tgt'}, use_global_device_ids=true, to_apply=%region_29.0 | all-reduce | flops 1024 | bytes 8192 | tf_op jit(solution)/shard_map/psum | solution.py:14
  895.8 0.0 copy-done.2
  895.8 0.0 copy-done
  895.8 0.0 copy-start.1
  895.8 16.5 %fusion = f32[1024,384]{1,0:T(8,128)} fusion(f32[1024,384]{0,1:T(8,128)S(1)} %copy-done, f32[1024,1024]{0,1:T(8,128)} %get-tuple-element.3, f32[1024]{0:T(1024)S(1)} %log_add_fusion, f32[1024]{0:T(1024)S(1)} %add_multiply_fusion), kind=kOutput, calls=%fused_computation | convolution fusion | flops 4834983936 | bytes 7348224 | tf_op jit(solution)/shard_map/dot_general | solution.py:49
  912.3 0.0 all-reduce.2.cloned.1.call-update
  912.3 161.9 %all-reduce.2.cloned.1.call-done = f32[1024,384]{1,0:T(8,128)} async-done(((f32[1024,384]{1,0:T(8,128)}), f32[1024,384]{1,0:T(8,128)}) %all-reduce.2.cloned.1.call-update) | async-done | bytes 1572880 | tf_op jit(solution)/shard_map/psum | solution.py:48
  1074.2 0.0 copy-done.1
  1074.2 1.4 dynamic-slice_subtract_fusion
  (7 shorter events, 0.1 us)
Async XLA Ops:
  7.2 48.6 %all-gather.5.cloned.1.call-start = ((), (), s32[]{:S(2)}) async-start(), calls=%async_computation.1 | async-start | bytes 1671168 | tf_op jit(solution)/shard_map/all_gather | solution.py:27
  7.9 133.6 %all-gather.3.cloned.1.call-start = ((), (), s32[]{:S(2)}) async-start(), calls=%async_computation | async-start | bytes 1622016 | tf_op jit(solution)/shard_map/all_gather | solution.py:26
  8.6 1065.6 %all-reduce.2.cloned.1.call-start = ((), (), s32[]{:S(2)}) async-start(), calls=%async_computation.2 | async-start | bytes 3145728 | tf_op jit(solution)/shard_map/psum | solution.py:48
  748.6 147.2 %copy-start.2 = (f32[1024]{0:T(1024)}, f32[1024]{0:T(1024)S(1)}, u32[]{:S(2)}) copy-start(f32[1024]{0:T(1024)S(1)} %add_multiply_fusion) | copy-start | bytes 12292
  748.6 147.2 %copy-start = (f32[1024,384]{0,1:T(8,128)S(1)}, f32[1024,384]{0,1:T(8,128)}, u32[]{:S(2)}) copy-start(f32[1024,384]{0,1:T(8,128)} %all-gather.5.cloned.1.call-done) | copy-start | bytes 4718596
  895.8 178.4 %copy-start.1 = (f32[32,384]{1,0:T(8,128)S(1)}, f32[32,384]{1,0:T(8,128)}, u32[]{:S(2)}) copy-start(f32[32,384]{1,0:T(8,128)} %param.2) | copy-start | bytes 147460
Sparse Core Ops, SparseCore 0:
  10.1 45.5 all-gather.4
  58.9 82.5 all-gather.2
  912.5 161.7 all-reduce.1
where the time goes:
time: 1080 us
  blocking collectives  704 us (65%)
  waiting for transfers between devices  294 us (27%)
  other arithmetic  42.6 us (4%)
  matrix products  27 us (2%)
  between operations  13.9 us (1%)
    pmax x4, blocking collectives, row_merge(): top = lax.pmax(local_top, 'tgt')  287 us
    psum x4, blocking collectives, row_merge(): total = lax.psum(jnp.sum(jnp.exp(z_tile - top[:, None]), axis=1), 'tgt')  279 us
    psum x1, waiting for transfers between devices, per_device(): lax.psum(jnp.dot(weight, target_rows, precision=lax.Precision.HIGHEST, pr...  162 us
    all_gather x1, waiting for transfers between devices, per_device(): source_rows = lax.all_gather(noise, 'tgt', axis=0, tiled=True)  84.2 us
    psum x3, blocking collectives, col_merge(): total = lax.psum(jnp.sum(jnp.exp(z_tile - top[None, :]), axis=0), 'src')  70.7 us
    pmax x3, blocking collectives, col_merge(): top = lax.pmax(local_top, 'src')  67.7 us
    all_gather x1, waiting for transfers between devices, per_device(): target_rows = lax.all_gather(data, 'src', axis=1, tiled=True)  47 us
  transfers between devices with their start and end apart: 3, of which 3 were waited for; matrix products, arithmetic and copies ran while one was open for 0% of the time, Pallas kernels for 0%

commit v1 on v0

--- a/solution.py
+++ b/solution.py
@@ -23,7 +23,9 @@
 
 
 def per_device(noise, data):
-    source_rows = lax.all_gather(noise, "tgt", axis=0, tiled=True)
+    source_rows = jnp.concatenate(
+        lax.all_to_all(jnp.stack([noise] * lax.axis_size("tgt")), "tgt", 0, 0), axis=0
+    )
     target_rows = lax.all_gather(data, "src", axis=1, tiled=True)
     feat_width = source_rows.shape[1]
     src_total = source_rows.shape[0] * lax.axis_size("src")

time: 1080 us -> 1000 us (0.926)
  waiting for transfers between devices: 294 us -> 200 us
  starting transfers between devices: 0.11 us -> 13.2 us
    all_gather x1 -> x0, waiting for transfers between devices: 84.2 us -> none  [per_device(): source_rows = lax.all_gather(noise, 'tgt', axis=0, tiled=True)]
    all_gather x1, waiting for transfers between devices: 47 us -> 32.3 us  [per_device(): target_rows = lax.all_gather(data, 'src', axis=1, tiled=True)]
    all_to_all x0 -> x1, starting transfers between devices: none -> 13.2 us  [per_device(): lax.all_to_all(jnp.stack([noise] * lax.axis_size('tgt')), 'tgt', 0, 0)]
where the time goes in v1:
time: 1000 us
  blocking collectives  705 us (70%)
  waiting for transfers between devices  200 us (20%)
  other arithmetic  41.2 us (4%)
  matrix products  26.5 us (3%)
  between operations  14.2 us (1%)
  starting transfers between devices  13.2 us (1%)
    pmax x4, blocking collectives, row_merge(): top = lax.pmax(local_top, 'tgt')  287 us
    psum x4, blocking collectives, row_merge(): total = lax.psum(jnp.sum(jnp.exp(z_tile - top[:, None]), axis=1), 'tgt')  279 us
    psum x1, waiting for transfers between devices, per_device(): lax.psum(jnp.dot(weight, target_rows, precision=lax.Precision.HIGHEST, pr...  162 us
    psum x3, blocking collectives, col_merge(): total = lax.psum(jnp.sum(jnp.exp(z_tile - top[None, :]), axis=0), 'src')  71 us
    pmax x3, blocking collectives, col_merge(): top = lax.pmax(local_top, 'src')  67.8 us
    all_gather x1, waiting for transfers between devices, per_device(): target_rows = lax.all_gather(data, 'src', axis=1, tiled=True)  32.3 us
  transfers between devices with their start and end apart: 3, of which 3 were waited for; matrix products, arithmetic and copies ran while one was open for 0% of the time, Pallas kernels for 0%

profile of v1, /device:TPU:8, one launch (start us, length us, event | category | flops | bytes accessed | tf_op | source)
XLA Modules:
  0.0 1002.2 jit_solution(17835513098961187194)
XLA Ops:
  7.2 0.0 all-gather.2.cloned.1.call-start
  7.2 0.7 all-gather.2.cloned.1.call-update
  7.9 2.1 stack.2
  10.0 13.2 %all-to-all-start = ((f32[32,32,384]{2,1,0:T(8,128)}), f32[32,32,384]{2,1,0:T(8,128)S(1)}, u32[]{:S(2)}, u32[]{:S(2)}) async-start(f32[32,32,384]{2,1,0:T(8,128)} %stack.2), calls=%async_computation | async-start | bytes 3145728 | tf_op jit(solution)/shard_map/all_to_all | solution.py:27
  23.2 0.0 all-reduce.2.cloned.1.call-start
  23.3 32.3 %all-gather.2.cloned.1.call-done = f32[1024,384]{0,1:T(8,128)} async-done(((f32[1024,24]{0,1:T(8,128)}), f32[1024,384]{0,1:T(8,128)}) %all-gather.2.cloned.1.call-update) | async-done | bytes 1572880 | tf_op jit(solution)/shard_map/all_gather | solution.py:29
  55.6 1.5 multiply_reduce_fusion
  57.1 5.4 all-to-all-done
  62.5 0.2 multiply_reduce_fusion.1
  62.8 0.1 add.73
  62.8 10.0 fusion.3
  72.8 72.3 %pmax.49 = f32[1024]{0:T(1024)S(1)} all-reduce(f32[1024]{0:T(1024)S(1)} %get-tuple-element.2), channel_id=1, replica_groups=mesh['src'=16,'tgt'=32] {'tgt'}, use_global_device_ids=true, to_apply=%region_3.0 | all-reduce | flops 1024 | bytes 8192 | tf_op jit(solution)/shard_map/pmax | solution.py:13
  145.1 3.0 exponential_reduce_fusion.6
  148.2 69.6 %psum.56 = f32[1024]{0:T(1024)S(1)} all-reduce(f32[1024]{0:T(1024)S(1)} %exponential_reduce_fusion.6), channel_id=1, replica_groups=mesh['src'=16,'tgt'=32] {'tgt'}, use_global_device_ids=true, to_apply=%region_5.0 | all-reduce | flops 1024 | bytes 8192 | tf_op jit(solution)/shard_map/psum | solution.py:14
  217.8 2.7 fusion.4
  220.5 20.7 %pmax.50 = f32[1024]{0:T(1024)S(1)} all-reduce(f32[1024]{0:T(1024)S(1)} %fusion.4), channel_id=1, replica_groups=mesh['src'=16,'tgt'=32] {'src'}, use_global_device_ids=true, to_apply=%region_7.0 | all-reduce | flops 1024 | bytes 8192 | tf_op jit(solution)/shard_map/pmax | solution.py:20
  241.2 3.2 exponential_reduce_fusion.5
  244.3 23.9 %psum.57 = f32[1024]{0:T(1024)S(1)} all-reduce(f32[1024]{0:T(1024)S(1)} %exponential_reduce_fusion.5), channel_id=1, replica_groups=mesh['src'=16,'tgt'=32] {'src'}, use_global_device_ids=true, to_apply=%region_9.0 | all-reduce | flops 1024 | bytes 8192 | tf_op jit(solution)/shard_map/psum | solution.py:21
  268.2 2.7 fusion.5
  270.9 71.7 %pmax.51 = f32[1024]{0:T(1024)S(1)} all-reduce(f32[1024]{0:T(1024)S(1)} %fusion.5), channel_id=1, replica_groups=mesh['src'=16,'tgt'=32] {'tgt'}, use_global_device_ids=true, to_apply=%region_11.0 | all-reduce | flops 1024 | bytes 8192 | tf_op jit(solution)/shard_map/pmax | solution.py:13
  342.6 3.1 exponential_reduce_fusion.4
  345.7 69.6 %psum.58 = f32[1024]{0:T(1024)S(1)} all-reduce(f32[1024]{0:T(1024)S(1)} %exponential_reduce_fusion.4), channel_id=1, replica_groups=mesh['src'=16,'tgt'=32] {'tgt'}, use_global_device_ids=true, to_apply=%region_13.0 | all-reduce | flops 1024 | bytes 8192 | tf_op jit(solution)/shard_map/psum | solution.py:14
  415.3 2.7 fusion.6
  418.0 23.6 %pmax.52 = f32[1024]{0:T(1024)S(1)} all-reduce(f32[1024]{0:T(1024)S(1)} %fusion.6), channel_id=1, replica_groups=mesh['src'=16,'tgt'=32] {'src'}, use_global_device_ids=true, to_apply=%region_15.0 | all-reduce | flops 1024 | bytes 8192 | tf_op jit(solution)/shard_map/pmax | solution.py:20
  441.5 3.2 exponential_reduce_fusion.3
  444.7 23.6 %psum.59 = f32[1024]{0:T(1024)S(1)} all-reduce(f32[1024]{0:T(1024)S(1)} %exponential_reduce_fusion.3), channel_id=1, replica_groups=mesh['src'=16,'tgt'=32] {'src'}, use_global_device_ids=true, to_apply=%region_17.0 | all-reduce | flops 1024 | bytes 8192 | tf_op jit(solution)/shard_map/psum | solution.py:21
  468.3 2.7 fusion.7
  470.9 71.8 %pmax.53 = f32[1024]{0:T(1024)S(1)} all-reduce(f32[1024]{0:T(1024)S(1)} %fusion.7), channel_id=1, replica_groups=mesh['src'=16,'tgt'=32] {'tgt'}, use_global_device_ids=true, to_apply=%region_19.0 | all-reduce | flops 1024 | bytes 8192 | tf_op jit(solution)/shard_map/pmax | solution.py:13
  542.7 3.1 exponential_reduce_fusion.2
  545.8 69.7 %psum.60 = f32[1024]{0:T(1024)S(1)} all-reduce(f32[1024]{0:T(1024)S(1)} %exponential_reduce_fusion.2), channel_id=1, replica_groups=mesh['src'=16,'tgt'=32] {'tgt'}, use_global_device_ids=true, to_apply=%region_21.0 | all-reduce | flops 1024 | bytes 8192 | tf_op jit(solution)/shard_map/psum | solution.py:14
  615.5 2.7 fusion.8
  618.2 23.6 %pmax.54 = f32[1024]{0:T(1024)S(1)} all-reduce(f32[1024]{0:T(1024)S(1)} %fusion.8), channel_id=1, replica_groups=mesh['src'=16,'tgt'=32] {'src'}, use_global_device_ids=true, to_apply=%region_23.0 | all-reduce | flops 1024 | bytes 8192 | tf_op jit(solution)/shard_map/pmax | solution.py:20
  641.7 3.2 exponential_reduce_fusion.1
  644.9 23.6 %psum.61 = f32[1024]{0:T(1024)S(1)} all-reduce(f32[1024]{0:T(1024)S(1)} %exponential_reduce_fusion.1), channel_id=1, replica_groups=mesh['src'=16,'tgt'=32] {'src'}, use_global_device_ids=true, to_apply=%region_25.0 | all-reduce | flops 1024 | bytes 8192 | tf_op jit(solution)/shard_map/psum | solution.py:21
  668.5 0.0 copy-start.2
  668.5 0.0 copy-start
  668.5 2.8 fusion.9
  671.3 71.6 %pmax.55 = f32[1024]{0:T(1024)S(1)} all-reduce(f32[1024]{0:T(1024)S(1)} %fusion.9), channel_id=1, replica_groups=mesh['src'=16,'tgt'=32] {'tgt'}, use_global_device_ids=true, to_apply=%region_27.0 | all-reduce | flops 1024 | bytes 8192 | tf_op jit(solution)/shard_map/pmax | solution.py:13
  742.9 3.1 exponential_reduce_fusion
  746.0 69.7 %psum.62 = f32[1024]{0:T(1024)S(1)} all-reduce(f32[1024]{0:T(1024)S(1)} %exponential_reduce_fusion), channel_id=1, replica_groups=mesh['src'=16,'tgt'=32] {'tgt'}, use_global_device_ids=true, to_apply=%region_29.0 | all-reduce | flops 1024 | bytes 8192 | tf_op jit(solution)/shard_map/psum | solution.py:14
  815.6 0.0 copy-done.2
  815.6 0.0 copy-done
  815.6 0.0 copy-start.1
  815.7 16.5 %fusion = f32[1024,384]{1,0:T(8,128)} fusion(f32[1024,384]{0,1:T(8,128)S(1)} %copy-done, f32[1024,1024]{0,1:T(8,128)} %get-tuple-element.3, f32[1024]{0:T(1024)S(1)} %log_add_fusion, f32[1024]{0:T(1024)S(1)} %add_multiply_fusion), kind=kOutput, calls=%fused_computation | convolution fusion | flops 4834983936 | bytes 7348224 | tf_op jit(solution)/shard_map/dot_general | solution.py:51
  832.1 0.0 all-reduce.2.cloned.1.call-update
  832.2 161.7 %all-reduce.2.cloned.1.call-done = f32[1024,384]{1,0:T(8,128)} async-done(((f32[1024,384]{1,0:T(8,128)}), f32[1024,384]{1,0:T(8,128)}) %all-reduce.2.cloned.1.call-update) | async-done | bytes 1572880 | tf_op jit(solution)/shard_map/psum | solution.py:50
  993.9 0.0 copy-done.1
  993.9 1.4 dynamic-slice_subtract_fusion
  (7 shorter events, 0.1 us)
Async XLA Ops:
  7.2 48.4 %all-gather.2.cloned.1.call-start = ((), (), s32[]{:S(2)}) async-start(), calls=%async_computation.1 | async-start | bytes 1671168 | tf_op jit(solution)/shard_map/all_gather | solution.py:29
  10.0 52.5 %all-to-all-start = ((f32[32,32,384]{2,1,0:T(8,128)}), f32[32,32,384]{2,1,0:T(8,128)S(1)}, u32[]{:S(2)}, u32[]{:S(2)}) async-start(f32[32,32,384]{2,1,0:T(8,128)} %stack.2), calls=%async_computation | async-start | bytes 3145728 | tf_op jit(solution)/shard_map/all_to_all | solution.py:27
  23.2 970.7 %all-reduce.2.cloned.1.call-start = ((), (), s32[]{:S(2)}) async-start(), calls=%async_computation.2 | async-start | bytes 3145728 | tf_op jit(solution)/shard_map/psum | solution.py:50
  668.5 147.2 %copy-start.2 = (f32[1024]{0:T(1024)}, f32[1024]{0:T(1024)S(1)}, u32[]{:S(2)}) copy-start(f32[1024]{0:T(1024)S(1)} %add_multiply_fusion) | copy-start | bytes 12292
  668.5 147.2 %copy-start = (f32[1024,384]{0,1:T(8,128)S(1)}, f32[1024,384]{0,1:T(8,128)}, u32[]{:S(2)}) copy-start(f32[1024,384]{0,1:T(8,128)} %all-gather.2.cloned.1.call-done) | copy-start | bytes 4718596
  815.6 178.2 %copy-start.1 = (f32[32,384]{1,0:T(8,128)S(1)}, f32[32,384]{1,0:T(8,128)}, u32[]{:S(2)}) copy-start(f32[32,384]{1,0:T(8,128)} %param.2) | copy-start | bytes 147460
Sparse Core Ops, SparseCore 0:
  10.1 45.4 all-gather.1
  832.3 161.5 all-reduce.1
